TPU v7x, 128 devices: a whole 4x4x4 slice. The times are simulated.
128 devices in a mesh: ctx: 16 (over y, z_hi, core), ch: 2 (over z_lo), dp: 4 (over x).
Axes of the slice: x: 4, y: 4, z: 4 (z_hi: 2, z_lo: 2; z = z_hi * 2 + z_lo), core: 2. Of those that a mesh axis runs over, the one named last changes fastest.
Arguments:
- features: bfloat16 [32768, 3, 4096], P(('dp', 'ctx'), None, 'ch'), parts along dimension 0, may hold values from -6 to 6
- short_filter: float32 [3, 3, 4096], P(None, None, 'ch'), may hold values from -3.5 to 3.5
- mode_residue: float32 [16, 4096], P(None, 'ch'), may hold values from -0.18 to 0.18
- decay_mix: float32 [16, 4096], P(None, 'ch'), may hold values from 0 to 1
- skip_gain: float32 [4096], P('ch'), may hold values from 0.5 to 1.5
- counter: int32 [8], P('dp'), parts along dimension 0, may hold values from 0 to 1048575
- out_weight: bfloat16 [4096, 4096], P('ch'), may hold values from -0.09375 to 0.09375
Outputs:
- projected: bfloat16 [32768, 4096], P(('dp', 'ctx', 'ch')), parts along dimension 0
There are 4 independent parts, one for each index of `dp`. A program takes and returns all parts, laid end to end along the dimension named above; an argument that names none is the same for every part. Nothing has to cross between parts.
All inputs are finite; a program needn't handle non-finite values.
Results may differ from a plain program's by a relative error of at most 0.012.
Values may be sent and summed in bfloat16 or wider, within the bound.
No kernel may reach another device: no remote copies, remote signals or barrier semaphores. Data moves between devices by JAX's collectives and lax.ppermute only.
A program may use at most 256 MiB of HBM per device.

v0:
```python
import math
import jax
import jax.numpy as jnp
from jax import lax
from jax.sharding import PartitionSpec as P

SHORT = 3
keep_scale = 8.0 / 7.0
precise = lax.Precision.HIGHEST


def passed_along(value, axis, steps):
    count = lax.axis_size(axis)
    leading, last = (max(0, -steps), min(count, count - steps))
    return lax.ppermute(value, axis, [(source, source + steps) for source in range(leading, last)])


def keep_mask(hash_base, positions, channels):
    bits = (
        hash_base
        + positions[:, None] * jnp.int32(-1640531535)
        + channels[None, :] * jnp.int32(-2048144777)
    )
    bits = bits ^ lax.shift_right_logical(bits, jnp.full_like(bits, 16))
    bits = bits * jnp.int32(2146121005)
    bits = bits ^ lax.shift_right_logical(bits, jnp.full_like(bits, 15))
    bits = bits * jnp.int32(-2073254261)
    bits = bits ^ lax.shift_right_logical(bits, jnp.full_like(bits, 16))
    return lax.shift_right_logical(bits, jnp.full_like(bits, 29)) != 0


def rates_of(mix, length):
    return jnp.exp(-((1.0 - mix) * math.log(length) + mix * math.log(30.0)))


def contract(form, left, right):
    return jnp.einsum(form, left, right, precision=precise)


def trig_table(rows, cols, period):
    product = (
        jnp.arange(rows, dtype=jnp.int32)[:, None]
        * jnp.arange(cols, dtype=jnp.int32)[None, :]
        % period
    )
    angle = product.astype(jnp.float32) * (2.0 * math.pi / period)
    return (jnp.cos(angle), jnp.sin(angle))


def split_table(table):
    upper = table.astype(jnp.bfloat16)
    lower = (table - upper.astype(jnp.float32)).astype(jnp.bfloat16)
    return (upper, lower)


def narrow_section(table, grid):
    upper, lower = split_table(table)
    first = jnp.einsum("ka,abc->kbc", upper, grid, preferred_element_type=jnp.float32)
    return first + jnp.einsum("ka,abc->kbc", lower, grid, preferred_element_type=jnp.float32)


def forward_dft(grid, tables):
    cos_outer, sin_outer, twist_cos, twist_sin, cos_inner, sin_inner = tables
    first_real = narrow_section(cos_outer, grid)
    first_imag = -narrow_section(sin_outer, grid)
    turned_real = first_real * twist_cos[:, :, None] + first_imag * twist_sin[:, :, None]
    turned_imag = first_imag * twist_cos[:, :, None] - first_real * twist_sin[:, :, None]
    out_real = contract("kbc,bm->kmc", turned_real, cos_inner) + contract(
        "kbc,bm->kmc", turned_imag, sin_inner
    )
    out_imag = contract("kbc,bm->kmc", turned_imag, cos_inner) - contract(
        "kbc,bm->kmc", turned_real, sin_inner
    )
    return (out_real, out_imag)


def inverse_dft(spec_real, spec_imag, tables):
    cos_outer, sin_outer, twist_cos, twist_sin, cos_inner, sin_inner = tables
    back_real = contract("kmc,bm->kbc", spec_real, cos_inner) - contract(
        "kmc,bm->kbc", spec_imag, sin_inner
    )
    back_imag = contract("kmc,bm->kbc", spec_imag, cos_inner) + contract(
        "kmc,bm->kbc", spec_real, sin_inner
    )
    turned_real = back_real * twist_cos[:, :, None] - back_imag * twist_sin[:, :, None]
    turned_imag = back_imag * twist_cos[:, :, None] + back_real * twist_sin[:, :, None]
    return contract("ka,kbc->abc", cos_outer, turned_real) - contract(
        "ka,kbc->abc", sin_outer, turned_imag
    )


def filter_spectrum(residue, mix, length, outer_len, inner_len):
    total_len = 2 * length
    rates = rates_of(mix, length)
    freq = (
        jnp.arange(outer_len, dtype=jnp.int32)[:, None]
        + outer_len * jnp.arange(inner_len, dtype=jnp.int32)[None, :]
    )
    angle = freq.astype(jnp.float32) * (2.0 * math.pi / total_len)
    sine_full = jnp.sin(angle)[:, :, None]
    sine_half = jnp.sin(0.5 * angle)[:, :, None]
    parity = (1 - 2 * (freq % 2)).astype(jnp.float32)[:, :, None]
    width = residue.shape[1]

    def add_mode(order_index, totals):
        rate = rates[order_index][None, None, :]
        factor = jnp.exp(-rate)
        numer = 1.0 - parity * jnp.exp(-rate * length)
        denom_real = -jnp.expm1(-rate) + factor * 2.0 * sine_half * sine_half
        denom_imag = factor * sine_full
        scale = (
            residue[order_index][None, None, :]
            * numer
            / (denom_real * denom_real + denom_imag * denom_imag)
        )
        return (totals[0] + scale * denom_real, totals[1] - scale * denom_imag)

    empty = jnp.zeros((outer_len, inner_len, width), jnp.float32)
    return lax.fori_loop(0, residue.shape[0], add_mode, (empty, empty))


def causal_fft(signal, residue, mix):
    length, width = signal.shape
    total_len = 2 * length
    inner_len = 128
    outer_len = total_len // inner_len
    half_outer = outer_len // 2
    cos_outer, sin_outer = trig_table(outer_len, half_outer, outer_len)
    twist_cos, twist_sin = trig_table(outer_len, inner_len, total_len)
    cos_inner, sin_inner = trig_table(inner_len, inner_len, inner_len)
    tables = (cos_outer, sin_outer, twist_cos, twist_sin, cos_inner, sin_inner)
    sig_real, sig_imag = forward_dft(signal.reshape(half_outer, inner_len, width), tables)
    tap_real, tap_imag = filter_spectrum(residue, mix, length, outer_len, inner_len)
    prod_real = sig_real * tap_real - sig_imag * tap_imag
    prod_imag = sig_real * tap_imag + sig_imag * tap_real
    return inverse_dft(prod_real, prod_imag, tables).reshape(length, width) / total_len


def body(features, short_filter, mode_residue, decay_mix, skip_gain, counter, out_weight):
    tok_rows = features.shape[0]
    local_width = features.shape[2]
    ctx_count = lax.axis_size("ctx")
    ctx_index = lax.axis_index("ctx")
    ch_index = lax.axis_index("ch")
    edge = passed_along(features[tok_rows - (SHORT - 1) :], "ctx", 1)
    joined = jnp.concatenate([edge, features], axis=0).astype(jnp.float32)
    filtered = jnp.zeros((tok_rows, 3, local_width), jnp.float32)
    for lag in range(SHORT):
        filtered = (
            filtered
            + short_filter[:, lag, :][None] * joined[SHORT - 1 - lag : SHORT - 1 - lag + tok_rows]
        )
    query = filtered[:, 0]
    keyed = filtered[:, 1]
    valued = filtered[:, 2]
    positions = counter[1] + ctx_index * tok_rows + jnp.arange(tok_rows, dtype=jnp.int32)
    channels = ch_index * local_width + jnp.arange(local_width, dtype=jnp.int32)
    gated = jnp.where(
        keep_mask(counter[0], positions, channels), keyed * valued * keep_scale, 0.0
    ).astype(jnp.bfloat16)
    gated_wide = gated.astype(jnp.float32)
    col_width = local_width // ctx_count
    columns = lax.all_to_all(gated, "ctx", split_axis=1, concat_axis=0, tiled=True)
    residue_part = lax.dynamic_slice_in_dim(mode_residue, ctx_index * col_width, col_width, 1)
    mix_part = lax.dynamic_slice_in_dim(decay_mix, ctx_index * col_width, col_width, 1)
    convolved = causal_fft(columns, residue_part, mix_part)
    conv_out = lax.all_to_all(convolved, "ctx", split_axis=0, concat_axis=1, tiled=True)
    long_out = conv_out + skip_gain[None, :] * gated_wide
    mixed = (query * long_out).astype(jnp.bfloat16)
    return lax.psum_scatter(
        jnp.dot(mixed, out_weight, preferred_element_type=jnp.float32).astype(jnp.bfloat16),
        "ch",
        scatter_dimension=0,
        tiled=True,
    )


def solution(mesh):
    placed = (
        P(("dp", "ctx"), None, "ch"),
        P(None, None, "ch"),
        P(None, "ch"),
        P(None, "ch"),
        P("ch"),
        P("dp"),
        P("ch", None),
    )
    return jax.shard_map(
        body, mesh=mesh, in_specs=placed, out_specs=P(("dp", "ctx", "ch"), None), check_vma=False
    )
```

profile of v0, /device:TPU:1, one launch (start us, length us, event | category | flops | bytes accessed | tf_op | source)
XLA Modules:
  0.0 655.3 jit_solution(195904797394615386)
XLA Ops:
  40.1 17.3 %fusion.17 = f32[512,3,2048]{0,2,1:T(8,128)S(1)} fusion(f32[514,3,2048]{0,2,1:T(8,128)} %maximum_convert_fusion, f32[3,2048]{1,0:T(4,128)S(1)} %get-tuple-element.271, f32[3,2048]{1,0:T(4,128)S(1)} %get-tuple-element.272, f32[3,2048]{1,0:T(4,128)S(1)} %bitcast.149), kind=kLoop, calls=%fused_computation.31 | loop fusion | flops 15728640 | bytes 50405376 | tf_op jit(solution)/shard_map/add | solution.py:150
  70.9 199.9 %while.19 = (s32[]{:T(128)}, f32[128,128,128]{2,1,0:T(8,128)}, f32[128,128,128]{2,1,0:T(8,128)}, f32[16,128]{1,0:T(8,128)S(1)}, f32[16,128]{1,0:T(8,128)S(1)}, /*index=5*/s32[128]{0:T(128)S(1)}, s32[]{:T(128)}, s32[]{:T(128)}) while((s32[]{:T(128)}, f32[128,128,128]{2,1,0:T(8,128)}, ...), condition=%wide.region_1.2_spmd.clone.clone.clone.clone, body=%wide.region_0.1_spmd.clone.clone.clone.clone.sunk | while | flops 35963392 | bytes 33956460 | solution.py:119
  81.4 12.1 %fusion.188 = (f32[128,128,128]{2,1,0:T(8,128)}, f32[128,128,128]{2,1,0:T(8,128)}) fusion(f32[128,128,128]{2,1,0:T(8,128)} %get-tuple-element.340, f32[128,128]{1,0:T(8,128)S(1)} %get-tuple-element.321, f32[128]{0:T(128)S(1)} %get-tuple-element.323, f32[128,128]{1,0:T(8,128)S(1)} %get-tuple-element.324, f32[128]{0:T(128)S(1)} %broadcast_multiply_fusion.2, ...), kind=kLoop, calls=%fused_computation.7.clone.1 | loop fusion | flops 35651584 | bytes 33753600 | tf_op jit(solution)/shard_map/while/body/eval_jaxpr/sub | solution.py:116
  94.1 12.1 %fusion.188 = (f32[128,128,128]{2,1,0:T(8,128)}, f32[128,128,128]{2,1,0:T(8,128)}) fusion(f32[128,128,128]{2,1,0:T(8,128)} %get-tuple-element.340, f32[128,128]{1,0:T(8,128)S(1)} %get-tuple-element.321, f32[128]{0:T(128)S(1)} %get-tuple-element.323, f32[128,128]{1,0:T(8,128)S(1)} %get-tuple-element.324, f32[128]{0:T(128)S(1)} %broadcast_multiply_fusion.2, ...), kind=kLoop, calls=%fused_computation.7.clone.1 | loop fusion | flops 35651584 | bytes 33753600 | tf_op jit(solution)/shard_map/while/body/eval_jaxpr/sub | solution.py:116
  106.8 12.1 %fusion.188 = (f32[128,128,128]{2,1,0:T(8,128)}, f32[128,128,128]{2,1,0:T(8,128)}) fusion(f32[128,128,128]{2,1,0:T(8,128)} %get-tuple-element.340, f32[128,128]{1,0:T(8,128)S(1)} %get-tuple-element.321, f32[128]{0:T(128)S(1)} %get-tuple-element.323, f32[128,128]{1,0:T(8,128)S(1)} %get-tuple-element.324, f32[128]{0:T(128)S(1)} %broadcast_multiply_fusion.2, ...), kind=kLoop, calls=%fused_computation.7.clone.1 | loop fusion | flops 35651584 | bytes 33753600 | tf_op jit(solution)/shard_map/while/body/eval_jaxpr/sub | solution.py:116
  132.1 12.1 %fusion.188 = (f32[128,128,128]{2,1,0:T(8,128)}, f32[128,128,128]{2,1,0:T(8,128)}) fusion(f32[128,128,128]{2,1,0:T(8,128)} %get-tuple-element.340, f32[128,128]{1,0:T(8,128)S(1)} %get-tuple-element.321, f32[128]{0:T(128)S(1)} %get-tuple-element.323, f32[128,128]{1,0:T(8,128)S(1)} %get-tuple-element.324, f32[128]{0:T(128)S(1)} %broadcast_multiply_fusion.2, ...), kind=kLoop, calls=%fused_computation.7.clone.1 | loop fusion | flops 35651584 | bytes 33753600 | tf_op jit(solution)/shard_map/while/body/eval_jaxpr/sub | solution.py:116
  144.7 12.1 %fusion.188 = (f32[128,128,128]{2,1,0:T(8,128)}, f32[128,128,128]{2,1,0:T(8,128)}) fusion(f32[128,128,128]{2,1,0:T(8,128)} %get-tuple-element.340, f32[128,128]{1,0:T(8,128)S(1)} %get-tuple-element.321, f32[128]{0:T(128)S(1)} %get-tuple-element.323, f32[128,128]{1,0:T(8,128)S(1)} %get-tuple-element.324, f32[128]{0:T(128)S(1)} %broadcast_multiply_fusion.2, ...), kind=kLoop, calls=%fused_computation.7.clone.1 | loop fusion | flops 35651584 | bytes 33753600 | tf_op jit(solution)/shard_map/while/body/eval_jaxpr/sub | solution.py:116
  157.4 12.1 %fusion.188 = (f32[128,128,128]{2,1,0:T(8,128)}, f32[128,128,128]{2,1,0:T(8,128)}) fusion(f32[128,128,128]{2,1,0:T(8,128)} %get-tuple-element.340, f32[128,128]{1,0:T(8,128)S(1)} %get-tuple-element.321, f32[128]{0:T(128)S(1)} %get-tuple-element.323, f32[128,128]{1,0:T(8,128)S(1)} %get-tuple-element.324, f32[128]{0:T(128)S(1)} %broadcast_multiply_fusion.2, ...), kind=kLoop, calls=%fused_computation.7.clone.1 | loop fusion | flops 35651584 | bytes 33753600 | tf_op jit(solution)/shard_map/while/body/eval_jaxpr/sub | solution.py:116
  170.1 12.1 %fusion.188 = (f32[128,128,128]{2,1,0:T(8,128)}, f32[128,128,128]{2,1,0:T(8,128)}) fusion(f32[128,128,128]{2,1,0:T(8,128)} %get-tuple-element.340, f32[128,128]{1,0:T(8,128)S(1)} %get-tuple-element.321, f32[128]{0:T(128)S(1)} %get-tuple-element.323, f32[128,128]{1,0:T(8,128)S(1)} %get-tuple-element.324, f32[128]{0:T(128)S(1)} %broadcast_multiply_fusion.2, ...), kind=kLoop, calls=%fused_computation.7.clone.1 | loop fusion | flops 35651584 | bytes 33753600 | tf_op jit(solution)/shard_map/while/body/eval_jaxpr/sub | solution.py:116
  182.7 12.1 %fusion.188 = (f32[128,128,128]{2,1,0:T(8,128)}, f32[128,128,128]{2,1,0:T(8,128)}) fusion(f32[128,128,128]{2,1,0:T(8,128)} %get-tuple-element.340, f32[128,128]{1,0:T(8,128)S(1)} %get-tuple-element.321, f32[128]{0:T(128)S(1)} %get-tuple-element.323, f32[128,128]{1,0:T(8,128)S(1)} %get-tuple-element.324, f32[128]{0:T(128)S(1)} %broadcast_multiply_fusion.2, ...), kind=kLoop, calls=%fused_computation.7.clone.1 | loop fusion | flops 35651584 | bytes 33753600 | tf_op jit(solution)/shard_map/while/body/eval_jaxpr/sub | solution.py:116
  195.4 12.1 %fusion.188 = (f32[128,128,128]{2,1,0:T(8,128)}, f32[128,128,128]{2,1,0:T(8,128)}) fusion(f32[128,128,128]{2,1,0:T(8,128)} %get-tuple-element.340, f32[128,128]{1,0:T(8,128)S(1)} %get-tuple-element.321, f32[128]{0:T(128)S(1)} %get-tuple-element.323, f32[128,128]{1,0:T(8,128)S(1)} %get-tuple-element.324, f32[128]{0:T(128)S(1)} %broadcast_multiply_fusion.2, ...), kind=kLoop, calls=%fused_computation.7.clone.1 | loop fusion | flops 35651584 | bytes 33753600 | tf_op jit(solution)/shard_map/while/body/eval_jaxpr/sub | solution.py:116
  208.1 12.1 %fusion.188 = (f32[128,128,128]{2,1,0:T(8,128)}, f32[128,128,128]{2,1,0:T(8,128)}) fusion(f32[128,128,128]{2,1,0:T(8,128)} %get-tuple-element.340, f32[128,128]{1,0:T(8,128)S(1)} %get-tuple-element.321, f32[128]{0:T(128)S(1)} %get-tuple-element.323, f32[128,128]{1,0:T(8,128)S(1)} %get-tuple-element.324, f32[128]{0:T(128)S(1)} %broadcast_multiply_fusion.2, ...), kind=kLoop, calls=%fused_computation.7.clone.1 | loop fusion | flops 35651584 | bytes 33753600 | tf_op jit(solution)/shard_map/while/body/eval_jaxpr/sub | solution.py:116
  220.7 12.1 %fusion.188 = (f32[128,128,128]{2,1,0:T(8,128)}, f32[128,128,128]{2,1,0:T(8,128)}) fusion(f32[128,128,128]{2,1,0:T(8,128)} %get-tuple-element.340, f32[128,128]{1,0:T(8,128)S(1)} %get-tuple-element.321, f32[128]{0:T(128)S(1)} %get-tuple-element.323, f32[128,128]{1,0:T(8,128)S(1)} %get-tuple-element.324, f32[128]{0:T(128)S(1)} %broadcast_multiply_fusion.2, ...), kind=kLoop, calls=%fused_computation.7.clone.1 | loop fusion | flops 35651584 | bytes 33753600 | tf_op jit(solution)/shard_map/while/body/eval_jaxpr/sub | solution.py:116
  258.7 12.1 %fusion.188 = (f32[128,128,128]{2,1,0:T(8,128)}, f32[128,128,128]{2,1,0:T(8,128)}) fusion(f32[128,128,128]{2,1,0:T(8,128)} %get-tuple-element.340, f32[128,128]{1,0:T(8,128)S(1)} %get-tuple-element.321, f32[128]{0:T(128)S(1)} %get-tuple-element.323, f32[128,128]{1,0:T(8,128)S(1)} %get-tuple-element.324, f32[128]{0:T(128)S(1)} %broadcast_multiply_fusion.2, ...), kind=kLoop, calls=%fused_computation.7.clone.1 | loop fusion | flops 35651584 | bytes 33753600 | tf_op jit(solution)/shard_map/while/body/eval_jaxpr/sub | solution.py:116
  299.6 17.5 %fusion.31 = f32[128,128,128]{2,0,1:T(8,128)} fusion(f32[128,128,128]{2,0,1:T(8,128)S(1)} %get-tuple-element.264), kind=kOutput, calls=%fused_computation.58 | convolution fusion | flops 3221454848 | bytes 16777216 | tf_op jit(solution)/shard_map/kbc,bm->kmc/dot_general | solution.py:37
  317.1 17.6 %fusion.33 = f32[128,128,128]{2,0,1:T(8,128)} fusion(f32[128,128,128]{2,0,1:T(8,128)S(1)} %get-tuple-element.264), kind=kOutput, calls=%fused_computation.60 | convolution fusion | flops 3221454848 | bytes 16777216 | tf_op jit(solution)/shard_map/kbc,bm->kmc/dot_general | solution.py:37
  334.7 17.7 %fusion.29 = f32[128,128,128]{2,0,1:T(8,128)} fusion(f32[128,128,128]{2,0,1:T(8,128)S(1)} %get-tuple-element.265), kind=kOutput, calls=%fused_computation.56 | convolution fusion | flops 3221454848 | bytes 16777216 | tf_op jit(solution)/shard_map/kbc,bm->kmc/dot_general | solution.py:37
  352.4 27.7 %fusion.25 = (f32[128,128,128]{2,1,0:T(8,128)}, f32[128,128,128]{2,1,0:T(8,128)}) fusion(f32[128,128,128]{2,1,0:T(8,128)} %get-tuple-element.149, f32[128,128,128]{2,1,0:T(8,128)} %get-tuple-element.148, f32[128,128,128]{2,0,1:T(8,128)} %fusion.31, f32[128,128,128]{2,0,1:T(8,128)} %fusion.33, f32[128,128,128]{2,0,1:T(8,128)} %fusion.29, ...), kind=kOutput, calls=%fused_computation.45 | convolution fusion | flops 3238232064 | bytes 67108864 | tf_op jit(solution)/shard_map/kbc,bm->kmc/dot_general | solution.py:37
  411.4 12.1 %fusion.72 = f32[128,128,128]{2,0,1:T(8,128)} fusion(f32[128,128,128]{2,1,0:T(8,128)} %get-tuple-element.263), kind=kOutput, calls=%fused_computation.116 | convolution fusion | flops 3221454848 | bytes 16777216 | tf_op jit(solution)/shard_map/kmc,bm->kbc/dot_general | solution.py:37
  423.5 33.1 %fusion.20 = f32[64,128,128]{2,0,1:T(8,128)} fusion(f32[128,128]{0,1:T(8,128)S(1)} %copy.72, f32[128,128]{0,1:T(8,128)S(1)} %copy.69, f32[128,128,128]{2,0,1:T(8,128)S(1)} %fusion.66, f32[128,128,128]{2,0,1:T(8,128)S(1)} %fusion.74, f32[128,128,128]{2,0,1:T(8,128)S(1)} %fusion.64, f32[128,128,128]{2,0,1:T(8,128)} %fusion.72), kind=kOutput, calls=%fused_computation.38 | convolution fusion | flops 1621213184 | bytes 37879808 | tf_op jit(solution)/shard_map/ka,kbc->abc/dot_general | solution.py:37
  456.6 33.1 %subtract_multiply_fusion = f32[64,128,128]{2,0,1:T(8,128)} fusion(f32[64,128,128]{2,0,1:T(8,128)} %fusion.20, f32[128,128]{0,1:T(8,128)S(1)} %copy.72, f32[128,128]{0,1:T(8,128)S(1)} %copy.69, f32[128,128,128]{2,0,1:T(8,128)S(1)} %fusion.66, f32[128,128,128]{2,0,1:T(8,128)S(1)} %fusion.74, f32[128,128,128]{2,0,1:T(8,128)S(1)} %fusion.64, ...), kind=kOutput, calls=%fused_computation.86 | convolution fusion | flops 1623310336 | bytes 42074112 | tf_op jit(solution)/shard_map/ka,kbc->abc/dot_general | solution.py:37
  503.7 53.0 %all-to-all-done.1 = f32[16,512,128]{2,1,0:T(8,128)} async-done(((f32[16,512,128]{2,1,0:T(8,128)}), f32[16,512,128]{2,1,0:T(8,128)}, u32[]{:S(2)}, u32[]{:S(2)}) %all-to-all-start.1) | async-done | bytes 4194336 | tf_op jit(solution)/shard_map/all_to_all | solution.py:167
  569.4 13.9 %convolution_convert_fusion = bf16[512,4096]{1,0:T(8,128)(2,1)} fusion(bf16[512,2048]{0,1:T(8,128)(2,1)S(1)} %fusion.45, bf16[2048,4096]{1,0:T(8,128)(2,1)} %param.15), kind=kOutput, calls=%fused_computation.69 | convolution fusion | flops 8592031744 | bytes 23068672 | tf_op jit(solution)/shard_map/dot_general | solution.py:171
  583.3 64.9 %reduce-scatter.2.cloned.1.call-done = bf16[256,4096]{1,0:T(8,128)(2,1)} async-done(((bf16[512,4096]{1,0:T(8,128)(2,1)}), bf16[256,4096]{1,0:T(8,128)(2,1)}) %reduce-scatter.2.cloned.1.call-update) | async-done | bytes 2097168 | tf_op jit(solution)/shard_map/reduce_scatter | solution.py:170
  (137 shorter events, 187.0 us)
Async XLA Ops:
  7.5 20.1 %collective-permute-start = (bf16[2,3,2048]{2,0,1:T(2,128)(2,1)S(1)}, bf16[2,3,2048]{2,0,1:T(2,128)(2,1)S(1)}, u32[]{:S(2)}, u32[]{:S(2)}) collective-permute-start(bf16[2,3,2048]{2,0,1:T(2,128)(2,1)S(1)} %slice.37), channel_id=1, source_target_pairs={{0,8},{8,16},{16,24},{24,32},{32,40},{40,48},{48,56},{56,64},{64,7... | collective-permute-start | bytes 73736 | tf_op jit(solution)/shard_map/ppermute | solution.py:15
  18.2 44.9 %copy-start.4 = (s32[512]{0:T(512)}, s32[512]{0:T(512)S(1)}, u32[]{:S(2)}) copy-start(s32[512]{0:T(512)S(1)} %multiply_add_fusion.2) | copy-start | bytes 6148
  57.4 4.5 copy-start
  66.0 205.5 %all-to-all-start = ((bf16[512,16,128]{0,2,1:T(8,128)(2,1)}), bf16[512,16,128]{0,2,1:T(8,128)(2,1)S(1)}, u32[]{:S(2)}, u32[]{:S(2)}) async-start(bf16[512,16,128]{0,2,1:T(8,128)(2,1)} %select_convert_fusion), calls=%async_computation | async-start | bytes 4194304 | tf_op jit(solution)/shard_map/all_to_all | solution.py:163
  271.5 1.3 copy-start.3
  299.6 35.1 %copy-start.2 = (f32[128,128,128]{2,0,1:T(8,128)}, f32[128,128,128]{2,0,1:T(8,128)S(1)}, u32[]{:S(2)}) copy-start(f32[128,128,128]{2,0,1:T(8,128)S(1)} %get-tuple-element.265) | copy-start | bytes 25165828
  380.2 11.7 %copy-start.1 = (f32[128,128,128]{2,1,0:T(8,128)S(1)}, f32[128,128,128]{2,1,0:T(8,128)}, u32[]{:S(2)}) copy-start(f32[128,128,128]{2,1,0:T(8,128)} %get-tuple-element.262) | copy-start | bytes 25165828
  496.2 66.0 %copy-start.5 = (s32[512]{0:T(512)S(1)}, s32[512]{0:T(512)}, u32[]{:S(2)}) copy-start(s32[512]{0:T(512)} %copy-done.4) | copy-start | bytes 6148
  496.3 66.0 %copy-start.6 = (f32[2048]{0:T(1024)S(1)}, f32[2048]{0:T(1024)}, u32[]{:S(2)}) copy-start(f32[2048]{0:T(1024)} %param.13) | copy-start | bytes 24580
  496.3 60.5 %all-to-all-start.1 = ((f32[16,512,128]{2,1,0:T(8,128)}), f32[16,512,128]{2,1,0:T(8,128)}, u32[]{:S(2)}, u32[]{:S(2)}) async-start(f32[16,512,128]{2,1,0:T(8,128)} %bitcast.146), calls=%async_computation.1 | async-start | bytes 8388608 | tf_op jit(solution)/shard_map/all_to_all | solution.py:167
  503.6 144.6 %reduce-scatter.2.cloned.1.call-start = ((), (), s32[]{:S(2)}) async-start(), calls=%async_computation.3 | async-start | bytes 6291456 | tf_op jit(solution)/shard_map/reduce_scatter | solution.py:170
Sparse Core Ops, SparseCore 0:
  583.5 64.7 reduce-scatter.1
where the time goes:
time: 663 us; the launch traced here: 655 us
  other arithmetic  241 us (36%)
  matrix products  228 us (34%)
  waiting for transfers between devices  118 us (18%)
  local copies, waits for them, and re-layouts  34.1 us (5%)
  starting transfers between devices  19.1 us (3%)
  between operations  14.5 us (2%)
    sub x16, other arithmetic, add_mode(): return (totals[0] + scale * denom_real, totals[1] - scale * denom_imag)  191 us
    dot_general x10, matrix products, contract(): return jnp.einsum(form, left, right, precision=precise)  190 us
    reduce_scatter x1, waiting for transfers between devices, body(): lax.psum_scatter(jnp.dot(mixed, out_weight, preferred_element_type=jnp.fl...  64.9 us
    all_to_all x1, waiting for transfers between devices, body(): lax.all_to_all(convolved, 'ctx', split_axis=0, concat_axis=1, tiled=True)  53 us
    add x1, other arithmetic, body(): filtered + short_filter[:, lag, :][None] * joined[SHORT - 1 - lag:SHORT -...  17.3 us
    dot_general x2, matrix products, narrow_section(): jnp.einsum('ka,abc->kbc', lower, grid, preferred_element_type=jnp.float32)  16.9 us
    unnamed x17, local copies, waits for them, and re-layouts  14.5 us
    dot_general x1, matrix products, body(): jnp.dot(mixed, out_weight, preferred_element_type=jnp.float32)  13.9 us
  transfers between devices with their start and end apart: 4, of which 2 were waited for; matrix products, arithmetic and copies ran while one was open for 32% of the time, Pallas kernels for 0%

commit v1 on v0

--- a/solution.py
+++ b/solution.py
@@ -164,7 +164,10 @@
     residue_part = lax.dynamic_slice_in_dim(mode_residue, ctx_index * col_width, col_width, 1)
     mix_part = lax.dynamic_slice_in_dim(decay_mix, ctx_index * col_width, col_width, 1)
     convolved = causal_fft(columns, residue_part, mix_part)
-    conv_out = lax.all_to_all(convolved, "ctx", split_axis=0, concat_axis=1, tiled=True)
+    conv_out = jnp.concatenate(
+        lax.all_to_all(jnp.stack(jnp.split(convolved, lax.axis_size("ctx"), axis=0)), "ctx", 0, 0),
+        axis=1,
+    )
     long_out = conv_out + skip_gain[None, :] * gated_wide
     mixed = (query * long_out).astype(jnp.bfloat16)
     return lax.psum_scatter(

time: 663 us -> 673 us (1.015)
  local copies, waits for them, and re-layouts: 34.1 us -> 43.7 us
    unnamed x17 -> x32, local copies, waits for them, and re-layouts: 14.5 us -> 25.3 us
where the time goes in v1:
time: 673 us; the launch traced here: 665 us
  other arithmetic  241 us (36%)
  matrix products  228 us (34%)
  waiting for transfers between devices  118 us (18%)
  local copies, waits for them, and re-layouts  43.7 us (6%)
  starting transfers between devices  19.1 us (3%)
  between operations  14.6 us (2%)
    sub x16, other arithmetic, add_mode(): return (totals[0] + scale * denom_real, totals[1] - scale * denom_imag)  191 us
    dot_general x10, matrix products, contract(): return jnp.einsum(form, left, right, precision=precise)  190 us
    reduce_scatter x1, waiting for transfers between devices, body(): lax.psum_scatter(jnp.dot(mixed, out_weight, preferred_element_type=jnp.fl...  64.9 us
    all_to_all x1, waiting for transfers between devices, body(): lax.all_to_all(jnp.stack(jnp.split(convolved, lax.axis_size('ctx'), axis=...  53 us
    unnamed x32, local copies, waits for them, and re-layouts  25.3 us
    add x1, other arithmetic, body(): filtered + short_filter[:, lag, :][None] * joined[SHORT - 1 - lag:SHORT -...  17.3 us
    dot_general x2, matrix products, narrow_section(): jnp.einsum('ka,abc->kbc', lower, grid, preferred_element_type=jnp.float32)  16.9 us
    dot_general x1, matrix products, body(): jnp.dot(mixed, out_weight, preferred_element_type=jnp.float32)  14 us
  transfers between devices with their start and end apart: 4, of which 2 were waited for; matrix products, arithmetic and copies ran while one was open for 32% of the time, Pallas kernels for 0%

profile of v1, /device:TPU:1, one launch (start us, length us, event | category | flops | bytes accessed | tf_op | source)
XLA Modules:
  0.0 665.0 jit_solution(1874849245776220313)
XLA Ops:
  40.0 17.3 %fusion.17 = f32[512,3,2048]{0,2,1:T(8,128)S(1)} fusion(f32[514,3,2048]{0,2,1:T(8,128)} %maximum_convert_fusion, f32[3,2048]{1,0:T(4,128)S(1)} %get-tuple-element.287, f32[3,2048]{1,0:T(4,128)S(1)} %get-tuple-element.288, f32[3,2048]{1,0:T(4,128)S(1)} %bitcast.211), kind=kLoop, calls=%fused_computation.31 | loop fusion | flops 15728640 | bytes 50405376 | tf_op jit(solution)/shard_map/add | solution.py:150
  70.8 199.8 %while.19 = (s32[]{:T(128)}, f32[128,128,128]{2,1,0:T(8,128)}, f32[128,128,128]{2,1,0:T(8,128)}, f32[16,128]{1,0:T(8,128)S(1)}, f32[16,128]{1,0:T(8,128)S(1)}, /*index=5*/s32[128]{0:T(128)S(1)}, s32[]{:T(128)}, s32[]{:T(128)}) while((s32[]{:T(128)}, f32[128,128,128]{2,1,0:T(8,128)}, ...), condition=%wide.region_1.2_spmd.clone.clone.clone.clone, body=%wide.region_0.1_spmd.clone.clone.clone.clone.sunk | while | flops 35963392 | bytes 33956460 | solution.py:119
  81.3 12.1 %fusion.189 = (f32[128,128,128]{2,1,0:T(8,128)}, f32[128,128,128]{2,1,0:T(8,128)}) fusion(f32[128,128,128]{2,1,0:T(8,128)} %get-tuple-element.356, f32[128,128]{1,0:T(8,128)S(1)} %get-tuple-element.337, f32[128]{0:T(128)S(1)} %get-tuple-element.339, f32[128,128]{1,0:T(8,128)S(1)} %get-tuple-element.340, f32[128]{0:T(128)S(1)} %broadcast_multiply_fusion.2, ...), kind=kLoop, calls=%fused_computation.7.clone.1 | loop fusion | flops 35651584 | bytes 33753600 | tf_op jit(solution)/shard_map/while/body/eval_jaxpr/sub | solution.py:116
  94.0 12.1 %fusion.189 = (f32[128,128,128]{2,1,0:T(8,128)}, f32[128,128,128]{2,1,0:T(8,128)}) fusion(f32[128,128,128]{2,1,0:T(8,128)} %get-tuple-element.356, f32[128,128]{1,0:T(8,128)S(1)} %get-tuple-element.337, f32[128]{0:T(128)S(1)} %get-tuple-element.339, f32[128,128]{1,0:T(8,128)S(1)} %get-tuple-element.340, f32[128]{0:T(128)S(1)} %broadcast_multiply_fusion.2, ...), kind=kLoop, calls=%fused_computation.7.clone.1 | loop fusion | flops 35651584 | bytes 33753600 | tf_op jit(solution)/shard_map/while/body/eval_jaxpr/sub | solution.py:116
  106.6 12.1 %fusion.189 = (f32[128,128,128]{2,1,0:T(8,128)}, f32[128,128,128]{2,1,0:T(8,128)}) fusion(f32[128,128,128]{2,1,0:T(8,128)} %get-tuple-element.356, f32[128,128]{1,0:T(8,128)S(1)} %get-tuple-element.337, f32[128]{0:T(128)S(1)} %get-tuple-element.339, f32[128,128]{1,0:T(8,128)S(1)} %get-tuple-element.340, f32[128]{0:T(128)S(1)} %broadcast_multiply_fusion.2, ...), kind=kLoop, calls=%fused_computation.7.clone.1 | loop fusion | flops 35651584 | bytes 33753600 | tf_op jit(solution)/shard_map/while/body/eval_jaxpr/sub | solution.py:116
  119.3 12.1 %fusion.189 = (f32[128,128,128]{2,1,0:T(8,128)}, f32[128,128,128]{2,1,0:T(8,128)}) fusion(f32[128,128,128]{2,1,0:T(8,128)} %get-tuple-element.356, f32[128,128]{1,0:T(8,128)S(1)} %get-tuple-element.337, f32[128]{0:T(128)S(1)} %get-tuple-element.339, f32[128,128]{1,0:T(8,128)S(1)} %get-tuple-element.340, f32[128]{0:T(128)S(1)} %broadcast_multiply_fusion.2, ...), kind=kLoop, calls=%fused_computation.7.clone.1 | loop fusion | flops 35651584 | bytes 33753600 | tf_op jit(solution)/shard_map/while/body/eval_jaxpr/sub | solution.py:116
  131.9 12.1 %fusion.189 = (f32[128,128,128]{2,1,0:T(8,128)}, f32[128,128,128]{2,1,0:T(8,128)}) fusion(f32[128,128,128]{2,1,0:T(8,128)} %get-tuple-element.356, f32[128,128]{1,0:T(8,128)S(1)} %get-tuple-element.337, f32[128]{0:T(128)S(1)} %get-tuple-element.339, f32[128,128]{1,0:T(8,128)S(1)} %get-tuple-element.340, f32[128]{0:T(128)S(1)} %broadcast_multiply_fusion.2, ...), kind=kLoop, calls=%fused_computation.7.clone.1 | loop fusion | flops 35651584 | bytes 33753600 | tf_op jit(solution)/shard_map/while/body/eval_jaxpr/sub | solution.py:116
  144.6 12.1 %fusion.189 = (f32[128,128,128]{2,1,0:T(8,128)}, f32[128,128,128]{2,1,0:T(8,128)}) fusion(f32[128,128,128]{2,1,0:T(8,128)} %get-tuple-element.356, f32[128,128]{1,0:T(8,128)S(1)} %get-tuple-element.337, f32[128]{0:T(128)S(1)} %get-tuple-element.339, f32[128,128]{1,0:T(8,128)S(1)} %get-tuple-element.340, f32[128]{0:T(128)S(1)} %broadcast_multiply_fusion.2, ...), kind=kLoop, calls=%fused_computation.7.clone.1 | loop fusion | flops 35651584 | bytes 33753600 | tf_op jit(solution)/shard_map/while/body/eval_jaxpr/sub | solution.py:116
  157.3 12.1 %fusion.189 = (f32[128,128,128]{2,1,0:T(8,128)}, f32[128,128,128]{2,1,0:T(8,128)}) fusion(f32[128,128,128]{2,1,0:T(8,128)} %get-tuple-element.356, f32[128,128]{1,0:T(8,128)S(1)} %get-tuple-element.337, f32[128]{0:T(128)S(1)} %get-tuple-element.339, f32[128,128]{1,0:T(8,128)S(1)} %get-tuple-element.340, f32[128]{0:T(128)S(1)} %broadcast_multiply_fusion.2, ...), kind=kLoop, calls=%fused_computation.7.clone.1 | loop fusion | flops 35651584 | bytes 33753600 | tf_op jit(solution)/shard_map/while/body/eval_jaxpr/sub | solution.py:116
  169.9 12.1 %fusion.189 = (f32[128,128,128]{2,1,0:T(8,128)}, f32[128,128,128]{2,1,0:T(8,128)}) fusion(f32[128,128,128]{2,1,0:T(8,128)} %get-tuple-element.356, f32[128,128]{1,0:T(8,128)S(1)} %get-tuple-element.337, f32[128]{0:T(128)S(1)} %get-tuple-element.339, f32[128,128]{1,0:T(8,128)S(1)} %get-tuple-element.340, f32[128]{0:T(128)S(1)} %broadcast_multiply_fusion.2, ...), kind=kLoop, calls=%fused_computation.7.clone.1 | loop fusion | flops 35651584 | bytes 33753600 | tf_op jit(solution)/shard_map/while/body/eval_jaxpr/sub | solution.py:116
  182.6 12.1 %fusion.189 = (f32[128,128,128]{2,1,0:T(8,128)}, f32[128,128,128]{2,1,0:T(8,128)}) fusion(f32[128,128,128]{2,1,0:T(8,128)} %get-tuple-element.356, f32[128,128]{1,0:T(8,128)S(1)} %get-tuple-element.337, f32[128]{0:T(128)S(1)} %get-tuple-element.339, f32[128,128]{1,0:T(8,128)S(1)} %get-tuple-element.340, f32[128]{0:T(128)S(1)} %broadcast_multiply_fusion.2, ...), kind=kLoop, calls=%fused_computation.7.clone.1 | loop fusion | flops 35651584 | bytes 33753600 | tf_op jit(solution)/shard_map/while/body/eval_jaxpr/sub | solution.py:116
  195.2 12.1 %fusion.189 = (f32[128,128,128]{2,1,0:T(8,128)}, f32[128,128,128]{2,1,0:T(8,128)}) fusion(f32[128,128,128]{2,1,0:T(8,128)} %get-tuple-element.356, f32[128,128]{1,0:T(8,128)S(1)} %get-tuple-element.337, f32[128]{0:T(128)S(1)} %get-tuple-element.339, f32[128,128]{1,0:T(8,128)S(1)} %get-tuple-element.340, f32[128]{0:T(128)S(1)} %broadcast_multiply_fusion.2, ...), kind=kLoop, calls=%fused_computation.7.clone.1 | loop fusion | flops 35651584 | bytes 33753600 | tf_op jit(solution)/shard_map/while/body/eval_jaxpr/sub | solution.py:116
  233.2 12.1 %fusion.189 = (f32[128,128,128]{2,1,0:T(8,128)}, f32[128,128,128]{2,1,0:T(8,128)}) fusion(f32[128,128,128]{2,1,0:T(8,128)} %get-tuple-element.356, f32[128,128]{1,0:T(8,128)S(1)} %get-tuple-element.337, f32[128]{0:T(128)S(1)} %get-tuple-element.339, f32[128,128]{1,0:T(8,128)S(1)} %get-tuple-element.340, f32[128]{0:T(128)S(1)} %broadcast_multiply_fusion.2, ...), kind=kLoop, calls=%fused_computation.7.clone.1 | loop fusion | flops 35651584 | bytes 33753600 | tf_op jit(solution)/shard_map/while/body/eval_jaxpr/sub | solution.py:116
  245.9 12.1 %fusion.189 = (f32[128,128,128]{2,1,0:T(8,128)}, f32[128,128,128]{2,1,0:T(8,128)}) fusion(f32[128,128,128]{2,1,0:T(8,128)} %get-tuple-element.356, f32[128,128]{1,0:T(8,128)S(1)} %get-tuple-element.337, f32[128]{0:T(128)S(1)} %get-tuple-element.339, f32[128,128]{1,0:T(8,128)S(1)} %get-tuple-element.340, f32[128]{0:T(128)S(1)} %broadcast_multiply_fusion.2, ...), kind=kLoop, calls=%fused_computation.7.clone.1 | loop fusion | flops 35651584 | bytes 33753600 | tf_op jit(solution)/shard_map/while/body/eval_jaxpr/sub | solution.py:116
  299.4 17.5 %fusion.31 = f32[128,128,128]{2,0,1:T(8,128)} fusion(f32[128,128,128]{2,0,1:T(8,128)S(1)} %get-tuple-element.264), kind=kOutput, calls=%fused_computation.58 | convolution fusion | flops 3221454848 | bytes 16777216 | tf_op jit(solution)/shard_map/kbc,bm->kmc/dot_general | solution.py:37
  316.9 17.6 %fusion.33 = f32[128,128,128]{2,0,1:T(8,128)} fusion(f32[128,128,128]{2,0,1:T(8,128)S(1)} %get-tuple-element.264), kind=kOutput, calls=%fused_computation.60 | convolution fusion | flops 3221454848 | bytes 16777216 | tf_op jit(solution)/shard_map/kbc,bm->kmc/dot_general | solution.py:37
  334.5 17.7 %fusion.29 = f32[128,128,128]{2,0,1:T(8,128)} fusion(f32[128,128,128]{2,0,1:T(8,128)S(1)} %get-tuple-element.265), kind=kOutput, calls=%fused_computation.56 | convolution fusion | flops 3221454848 | bytes 16777216 | tf_op jit(solution)/shard_map/kbc,bm->kmc/dot_general | solution.py:37
  352.3 27.7 %fusion.25 = (f32[128,128,128]{2,1,0:T(8,128)}, f32[128,128,128]{2,1,0:T(8,128)}) fusion(f32[128,128,128]{2,1,0:T(8,128)} %get-tuple-element.149, f32[128,128,128]{2,1,0:T(8,128)} %get-tuple-element.148, f32[128,128,128]{2,0,1:T(8,128)} %fusion.31, f32[128,128,128]{2,0,1:T(8,128)} %fusion.33, f32[128,128,128]{2,0,1:T(8,128)} %fusion.29, ...), kind=kOutput, calls=%fused_computation.45 | convolution fusion | flops 3238232064 | bytes 67108864 | tf_op jit(solution)/shard_map/kbc,bm->kmc/dot_general | solution.py:37
  411.2 12.1 %fusion.72 = f32[128,128,128]{2,0,1:T(8,128)} fusion(f32[128,128,128]{2,1,0:T(8,128)} %get-tuple-element.263), kind=kOutput, calls=%fused_computation.132 | convolution fusion | flops 3221454848 | bytes 16777216 | tf_op jit(solution)/shard_map/kmc,bm->kbc/dot_general | solution.py:37
  423.3 33.1 %fusion.20 = f32[64,128,128]{2,0,1:T(8,128)} fusion(f32[128,128]{0,1:T(8,128)S(1)} %copy.102, f32[128,128]{0,1:T(8,128)S(1)} %copy.99, f32[128,128,128]{2,0,1:T(8,128)S(1)} %fusion.66, f32[128,128,128]{2,0,1:T(8,128)S(1)} %fusion.74, f32[128,128,128]{2,0,1:T(8,128)S(1)} %fusion.64, f32[128,128,128]{2,0,1:T(8,128)} %fusion.72), kind=kOutput, calls=%fused_computation.38 | convolution fusion | flops 1621213184 | bytes 37879808 | tf_op jit(solution)/shard_map/ka,kbc->abc/dot_general | solution.py:37
  456.4 33.1 %subtract_multiply_fusion = f32[64,128,128]{2,0,1:T(8,128)} fusion(f32[64,128,128]{2,0,1:T(8,128)} %fusion.20, f32[128,128]{0,1:T(8,128)S(1)} %copy.102, f32[128,128]{0,1:T(8,128)S(1)} %copy.99, f32[128,128,128]{2,0,1:T(8,128)S(1)} %fusion.66, f32[128,128,128]{2,0,1:T(8,128)S(1)} %fusion.74, f32[128,128,128]{2,0,1:T(8,128)S(1)} %fusion.64, ...), kind=kOutput, calls=%fused_computation.86 | convolution fusion | flops 1623310336 | bytes 42074112 | tf_op jit(solution)/shard_map/ka,kbc->abc/dot_general | solution.py:37
  513.2 53.0 %all-to-all-done.1 = f32[16,512,128]{2,1,0:T(8,128)} async-done(((f32[16,512,128]{2,1,0:T(8,128)}), f32[16,512,128]{2,1,0:T(8,128)}, u32[]{:S(2)}, u32[]{:S(2)}) %all-to-all-start.1) | async-done | bytes 4194336 | tf_op jit(solution)/shard_map/all_to_all | solution.py:168
  579.0 14.0 %convolution_convert_fusion = bf16[512,4096]{1,0:T(8,128)(2,1)} fusion(bf16[512,2048]{0,1:T(8,128)(2,1)S(1)} %fusion.45, bf16[2048,4096]{1,0:T(8,128)(2,1)} %param.15), kind=kOutput, calls=%fused_computation.69 | convolution fusion | flops 8592031744 | bytes 23068672 | tf_op jit(solution)/shard_map/dot_general | solution.py:174
  593.0 64.9 %reduce-scatter.2.cloned.1.call-done = bf16[256,4096]{1,0:T(8,128)(2,1)} async-done(((bf16[512,4096]{1,0:T(8,128)(2,1)}), bf16[256,4096]{1,0:T(8,128)(2,1)}) %reduce-scatter.2.cloned.1.call-update) | async-done | bytes 2097168 | tf_op jit(solution)/shard_map/reduce_scatter | solution.py:173
  (169 shorter events, 196.5 us)
Async XLA Ops:
  7.5 20.0 %collective-permute-start = (bf16[2,3,2048]{2,0,1:T(2,128)(2,1)S(1)}, bf16[2,3,2048]{2,0,1:T(2,128)(2,1)S(1)}, u32[]{:S(2)}, u32[]{:S(2)}) collective-permute-start(bf16[2,3,2048]{2,0,1:T(2,128)(2,1)S(1)} %slice.53), channel_id=1, source_target_pairs={{0,8},{8,16},{16,24},{24,32},{32,40},{40,48},{48,56},{56,64},{64,7... | collective-permute-start | bytes 73736 | tf_op jit(solution)/shard_map/ppermute | solution.py:15
  18.1 44.8 %copy-start.4 = (s32[512]{0:T(512)}, s32[512]{0:T(512)S(1)}, u32[]{:S(2)}) copy-start(s32[512]{0:T(512)S(1)} %multiply_add_fusion.2) | copy-start | bytes 6148
  57.3 4.5 copy-start
  65.9 205.4 %all-to-all-start = ((bf16[512,16,128]{0,2,1:T(8,128)(2,1)}), bf16[512,16,128]{0,2,1:T(8,128)(2,1)S(1)}, u32[]{:S(2)}, u32[]{:S(2)}) async-start(bf16[512,16,128]{0,2,1:T(8,128)(2,1)} %select_convert_fusion), calls=%async_computation | async-start | bytes 4194304 | tf_op jit(solution)/shard_map/all_to_all | solution.py:163
  271.3 1.3 copy-start.3
  299.4 35.1 %copy-start.2 = (f32[128,128,128]{2,0,1:T(8,128)}, f32[128,128,128]{2,0,1:T(8,128)S(1)}, u32[]{:S(2)}) copy-start(f32[128,128,128]{2,0,1:T(8,128)S(1)} %get-tuple-element.265) | copy-start | bytes 25165828
  380.0 11.7 %copy-start.1 = (f32[128,128,128]{2,1,0:T(8,128)S(1)}, f32[128,128,128]{2,1,0:T(8,128)}, u32[]{:S(2)}) copy-start(f32[128,128,128]{2,1,0:T(8,128)} %get-tuple-element.262) | copy-start | bytes 25165828
  505.8 66.0 %copy-start.5 = (s32[512]{0:T(512)S(1)}, s32[512]{0:T(512)}, u32[]{:S(2)}) copy-start(s32[512]{0:T(512)} %copy-done.4) | copy-start | bytes 6148
  505.8 66.0 %copy-start.6 = (f32[2048]{0:T(1024)S(1)}, f32[2048]{0:T(1024)}, u32[]{:S(2)}) copy-start(f32[2048]{0:T(1024)} %param.13) | copy-start | bytes 24580
  505.8 60.5 %all-to-all-start.1 = ((f32[16,512,128]{2,1,0:T(8,128)}), f32[16,512,128]{2,1,0:T(8,128)}, u32[]{:S(2)}, u32[]{:S(2)}) async-start(f32[16,512,128]{2,1,0:T(8,128)} %bitcast_dynamic-update-slice_fusion), calls=%async_computation.1 | async-start | bytes 8388608 | tf_op jit(solution)/shard_map/all_to_all | solution.py:168
  513.2 144.7 %reduce-scatter.2.cloned.1.call-start = ((), (), s32[]{:S(2)}) async-start(), calls=%async_computation.3 | async-start | bytes 6291456 | tf_op jit(solution)/shard_map/reduce_scatter | solution.py:173
Sparse Core Ops, SparseCore 0:
  593.1 64.7 reduce-scatter.1
